TPU v7x, 32 devices: a whole 2x2x4 slice. The times are simulated.
32 devices in a mesh: dp: 8 (over y, x, core), mp: 4 (over z).
Axes of the slice: x: 2, y: 2, z: 4, core: 2. Of those that a mesh axis runs over, the one named last changes fastest.
Arguments:
- tokens: bfloat16 [128, 542, 768], P(('dp', 'mp')), may hold values from -6 to 6
- cotangent: bfloat16 [128, 542, 768], P(('dp', 'mp')), may hold values from -6 to 6
- kept_index: int32 [128, 268], P(('dp', 'mp')), may hold values from 0 to 541, as said below
- attention_weights: float32 [768, 3072], P(None, ('dp', 'mp')), may hold values from -0.4082483 to 0.4082483
- attention_first: float32 [768, 3072], P(None, ('dp', 'mp')), may hold values from -224 to 224
- attention_second: float32 [768, 3072], P(None, ('dp', 'mp')), may hold values from 1372.16 to 5488.64
- attention_average: float32 [768, 3072], P(None, ('dp', 'mp')), may hold values from -0.4082483 to 0.4082483
- feedforward_weights: float32 [2, 768, 3072], P(None, 'dp', 'mp'), may hold values from -0.14433757 to 0.14433757
- feedforward_first: float32 [2, 768, 3072], P(None, 'dp', 'mp'), may hold values from -448 to 448
- feedforward_second: float32 [2, 768, 3072], P(None, 'dp', 'mp'), may hold values from 5488.64 to 21954.56
- feedforward_average: float32 [2, 768, 3072], P(None, 'dp', 'mp'), may hold values from -0.14433757 to 0.14433757
- vector_weights: float32 [13, 768], replicated, may hold values from -1.2 to 1.3
- vector_first: float32 [13, 768], replicated, may hold values from -1024 to 1024
- vector_second: float32 [13, 768], replicated, may hold values from 34304 to 137216
- vector_average: float32 [13, 768], replicated, may hold values from -1.2 to 1.3
Outputs:
- block_output: bfloat16 [128, 542, 768], P(('dp', 'mp'))
- input_gradient: float32 [128, 542, 768], P(('dp', 'mp'))
- attention_gradient: float32 [768, 3072], P(None, ('dp', 'mp'))
- attention_first_new: float32 [768, 3072], P(None, ('dp', 'mp'))
- attention_second_new: float32 [768, 3072], P(None, ('dp', 'mp'))
- attention_weights_new: float32 [768, 3072], P(None, ('dp', 'mp'))
- attention_average_new: float32 [768, 3072], P(None, ('dp', 'mp'))
- attention_copy: bfloat16 [768, 3072], P(None, ('dp', 'mp'))
- feedforward_gradient: float32 [2, 768, 3072], P(None, 'dp', 'mp')
- feedforward_first_new: float32 [2, 768, 3072], P(None, 'dp', 'mp')
- feedforward_second_new: float32 [2, 768, 3072], P(None, 'dp', 'mp')
- feedforward_weights_new: float32 [2, 768, 3072], P(None, 'dp', 'mp')
- feedforward_average_new: float32 [2, 768, 3072], P(None, 'dp', 'mp')
- feedforward_copy: bfloat16 [2, 768, 3072], P(None, 'dp', 'mp')
- vector_gradient: float32 [13, 768], replicated
- vector_first_new: float32 [13, 768], replicated
- vector_second_new: float32 [13, 768], replicated
- vector_weights_new: float32 [13, 768], replicated
- vector_average_new: float32 [13, 768], replicated
- query_bias_gradient: float32 [768], replicated
Inputs may be any that keep to these rules, and one draw needn't show every extreme that they name: `kept_index`: for each image and each of its six crops in order, 197//2 (global crops) or 37//2 (local crops) distinct increasing positions inside that crop; the crop's first and last positions are always among them.
All inputs are finite; a program needn't handle non-finite values.
Results may differ from a plain program's by a relative error of at most 0.0098.
The roundings to bfloat16 on the way count: a program that leaves them out, or rounds other values in their place, can miss the bound.
Values may be sent and summed in bfloat16 or wider, within the bound.
A program may use at most 192 MiB of HBM per device.

v0:
```python
import jax
import jax.numpy as jnp
import numpy as np
from jax import lax
from jax.sharding import PartitionSpec as P

H = 12
HD = 64
FF = 3072
LG = 197
LL = 37
HIGHEST = lax.Precision.HIGHEST


def crop_labels():
    labels = [0] * (LG // 2) + [1] * (LG // 2)
    for crop in range(2, 6):
        labels = labels + [crop] * (LL // 2)
    return np.array(labels, np.int32)


def normalize(rows):
    center = rows - jnp.mean(rows, axis=-1, keepdims=True)
    spread = jnp.mean(center * center, axis=-1, keepdims=True)
    inverse = lax.rsqrt(spread + 1e-06)
    return (center * inverse, inverse)


def norm_backward(upstream, standard, inverse, gain):
    scaled = upstream * gain
    return inverse * (
        scaled
        - jnp.mean(scaled, axis=-1, keepdims=True)
        - standard * jnp.mean(scaled * standard, axis=-1, keepdims=True)
    )


def gelu_slope(inner):
    return (
        0.5 * (1.0 + lax.erf(inner * 0.7071067811865476))
        + inner * jnp.exp(-0.5 * inner * inner) * 0.3989422804014327
    )


def transpose_product(left, right):
    return lax.dot_general(
        left, right, (((0,), (0,)), ((), ())), preferred_element_type=jnp.float32
    )


def product_transposed(left, right):
    return lax.dot_general(
        left, right, (((1,), (1,)), ((), ())), preferred_element_type=jnp.float32
    )


def adamw(grad, first, second, master, average, rate, decay):
    first_new = 0.5 * first + 0.5 * grad
    second_new = 0.5 * second + 0.5 * grad * grad
    update = first_new / (jnp.sqrt(second_new) + 1e-08)
    master_new = master - rate * (update + decay * master)
    average_new = 0.9 * average + 0.1 * master_new
    return (first_new, second_new, master_new, average_new)


def per_device(
    tokens,
    cotangent,
    kept_index,
    attention_weights,
    attention_first,
    attention_second,
    attention_average,
    feedforward_weights,
    feedforward_first,
    feedforward_second,
    feedforward_average,
    vector_weights,
    vector_first,
    vector_second,
    vector_average,
):
    images, length = kept_index.shape
    width = tokens.shape[2]
    heads = H
    head_size = HD
    hidden = FF
    hidden_local = feedforward_weights.shape[2]
    rows_count = images * length
    labels = crop_labels()
    same_crop = jnp.asarray(labels[:, None] == labels[None, :])
    factor = head_size ** (-0.5)
    bf16 = jnp.bfloat16
    f32 = jnp.float32
    attention_full = lax.all_gather(
        attention_weights.astype(bf16), ("dp", "mp"), axis=1, tiled=True
    )
    feed_rows = lax.all_gather(feedforward_weights.astype(bf16), "dp", axis=1, tiled=True)
    first_bias = vector_weights[9:].reshape(hidden)
    bias_used = lax.dynamic_slice_in_dim(
        first_bias, lax.axis_index("mp") * hidden_local, hidden_local
    )
    tokens_float = tokens.astype(f32)
    kept_rows = jnp.take_along_axis(tokens_float, kept_index[:, :, None], axis=1).reshape(
        rows_count, width
    )
    standard_one, inverse_one = normalize(kept_rows)
    normed = (standard_one * vector_weights[0] + vector_weights[1]).astype(bf16)
    normed_float = normed.astype(f32)
    score = jax.nn.sigmoid(jnp.dot(normed_float, vector_weights[2], precision=HIGHEST))
    bias_three = jnp.concatenate(
        [vector_weights[3], jnp.zeros_like(vector_weights[3]), vector_weights[4]]
    )
    project = (
        jnp.dot(normed, attention_full[:, : 3 * width], preferred_element_type=f32) + bias_three
    ).astype(bf16)
    query = project[:, :width].reshape(images, length, heads, head_size)
    keys = project[:, width : 2 * width].reshape(images, length, heads, head_size)
    values = project[:, 2 * width :].reshape(images, length, heads, head_size)
    scores = factor * jnp.einsum("ikhd,ijhd->ihkj", query, keys, preferred_element_type=f32)
    scores = jnp.where(same_crop, scores, -1000000000.0)
    total = jax.nn.logsumexp(scores, axis=-1, keepdims=True)
    probs_low = jnp.exp(scores - total).astype(bf16)
    mixed = (
        jnp.einsum("ihkj,ijhd->ikhd", probs_low, values, preferred_element_type=f32)
        .reshape(rows_count, width)
        .astype(bf16)
    )
    branch = (
        jnp.dot(mixed, attention_full[:, 3 * width :], preferred_element_type=f32)
        + vector_weights[5]
    )
    residual = kept_rows + score[:, None] * branch
    standard_two, inverse_two = normalize(residual)
    normed_two = (standard_two * vector_weights[6] + vector_weights[7]).astype(bf16)
    rows_all = lax.all_gather(normed_two, "mp", axis=0, tiled=True)
    inner = jnp.dot(rows_all, feed_rows[0], preferred_element_type=f32) + bias_used
    activated = jax.nn.gelu(inner, approximate=False).astype(bf16)
    piece = activated
    output = lax.psum_scatter(
        product_transposed(piece, feed_rows[1]).astype(jnp.bfloat16),
        "mp",
        scatter_dimension=0,
        tiled=True,
    ).astype(jnp.float32)
    result = residual + output + vector_weights[8]
    image_index = jnp.arange(images)[:, None]
    block_output = tokens.at[image_index, kept_index].set(
        result.reshape(images, length, width).astype(bf16)
    )
    cot_float = cotangent.astype(f32)
    cot_kept = jnp.take_along_axis(cotangent, kept_index[:, :, None], axis=1).reshape(
        rows_count, width
    )
    cot_all = lax.all_gather(cot_kept, "mp", axis=0, tiled=True)
    down_grad = transpose_product(cot_all, activated)
    active_grad = jnp.dot(cot_all, feed_rows[1], preferred_element_type=f32)
    inner_grad = (active_grad * gelu_slope(inner)).astype(bf16)
    up_grad = transpose_product(rows_all, inner_grad)
    bias_grad_local = jnp.sum(inner_grad.astype(f32), axis=0)
    piece = inner_grad
    normed_two_grad = lax.psum_scatter(
        product_transposed(piece, feed_rows[0]), "mp", scatter_dimension=0, tiled=True
    )
    cot_rows = cot_kept.astype(f32)
    residual_grad = cot_rows + norm_backward(
        normed_two_grad, standard_two, inverse_two, vector_weights[6]
    )
    gain_two_grad = jnp.sum(normed_two_grad * standard_two, axis=0)
    shift_two_grad = jnp.sum(normed_two_grad, axis=0)
    second_bias_grad = jnp.sum(cot_rows, axis=0)
    branch_grad = (score[:, None] * residual_grad).astype(bf16)
    router_grad = jnp.sum(residual_grad * branch, axis=1) * score * (1.0 - score)
    router_weight_grad = jnp.dot(router_grad, normed_float, precision=HIGHEST)
    out_grad = transpose_product(mixed, branch_grad)
    out_bias_grad = jnp.sum(branch_grad.astype(f32), axis=0)
    mixed_grad = product_transposed(branch_grad, attention_full[:, 3 * width :]).astype(bf16)
    mixed_grad = mixed_grad.reshape(images, length, heads, head_size)
    scores_again = factor * jnp.einsum("ikhd,ijhd->ihkj", query, keys, preferred_element_type=f32)
    probs = jnp.exp(jnp.where(same_crop, scores_again, -1000000000.0) - total)
    probs_grad = jnp.einsum("ikhd,ijhd->ihkj", mixed_grad, values, preferred_element_type=f32)
    inner_sum = jnp.sum(probs * probs_grad, axis=-1, keepdims=True)
    scores_grad = (probs * (probs_grad - inner_sum)).astype(bf16)
    query_grad = factor * jnp.einsum(
        "ihkj,ijhd->ikhd", scores_grad, keys, preferred_element_type=f32
    )
    key_grad = factor * jnp.einsum(
        "ihkj,ikhd->ijhd", scores_grad, query, preferred_element_type=f32
    )
    value_grad = jnp.einsum("ihkj,ikhd->ijhd", probs_low, mixed_grad, preferred_element_type=f32)
    project_grad = jnp.concatenate(
        [
            query_grad.reshape(rows_count, width),
            key_grad.reshape(rows_count, width),
            value_grad.reshape(rows_count, width),
        ],
        axis=1,
    ).astype(bf16)
    in_grad = transpose_product(normed, project_grad)
    project_float = project_grad.astype(f32)
    query_bias_grad = jnp.sum(project_float[:, :width], axis=0)
    value_bias_grad = jnp.sum(project_float[:, 2 * width :], axis=0)
    normed_grad = router_grad[:, None] * vector_weights[2] + product_transposed(
        project_grad, attention_full[:, : 3 * width]
    )
    gain_one_grad = jnp.sum(normed_grad * standard_one, axis=0)
    shift_one_grad = jnp.sum(normed_grad, axis=0)
    kept_grad = residual_grad + norm_backward(
        normed_grad, standard_one, inverse_one, vector_weights[0]
    )
    input_gradient = cot_float.at[image_index, kept_index].set(
        kept_grad.reshape(images, length, width)
    )
    attention_local = jnp.concatenate([in_grad, out_grad], axis=1)
    attention_gradient = lax.psum_scatter(
        attention_local, ("dp", "mp"), scatter_dimension=1, tiled=True
    )
    feed_local = jnp.stack([up_grad, down_grad])
    bias_full = lax.dynamic_update_slice_in_dim(
        jnp.zeros((hidden,), f32), bias_grad_local, lax.axis_index("mp") * hidden_local, 0
    )
    feedforward_gradient = lax.psum_scatter(feed_local, "dp", scatter_dimension=1, tiled=True)
    vector_local = jnp.concatenate(
        [
            jnp.stack(
                [
                    gain_one_grad,
                    shift_one_grad,
                    router_weight_grad,
                    query_bias_grad,
                    value_bias_grad,
                    out_bias_grad,
                    gain_two_grad,
                    shift_two_grad,
                    second_bias_grad,
                ]
            ),
            bias_full.reshape(-1, width),
        ],
        axis=0,
    )
    vector_gradient = lax.psum(vector_local, ("dp", "mp"))
    attention_new = adamw(
        attention_gradient,
        attention_first,
        attention_second,
        attention_weights,
        attention_average,
        0.02,
        0.05,
    )
    feedforward_new = adamw(
        feedforward_gradient,
        feedforward_first,
        feedforward_second,
        feedforward_weights,
        feedforward_average,
        0.02,
        0.05,
    )
    vector_new = adamw(
        vector_gradient, vector_first, vector_second, vector_weights, vector_average, 0.2, 0.0
    )
    return (
        block_output,
        input_gradient,
        attention_gradient,
        attention_new[0],
        attention_new[1],
        attention_new[2],
        attention_new[3],
        attention_new[2].astype(bf16),
        feedforward_gradient,
        feedforward_new[0],
        feedforward_new[1],
        feedforward_new[2],
        feedforward_new[3],
        feedforward_new[2].astype(bf16),
        vector_gradient,
        vector_new[0],
        vector_new[1],
        vector_new[2],
        vector_new[3],
        vector_gradient[3],
    )


def solution(mesh):
    in_specs = (
        P(("dp", "mp"), None, None),
        P(("dp", "mp"), None, None),
        P(("dp", "mp"), None),
        P(None, ("dp", "mp")),
        P(None, ("dp", "mp")),
        P(None, ("dp", "mp")),
        P(None, ("dp", "mp")),
        P(None, "dp", "mp"),
        P(None, "dp", "mp"),
        P(None, "dp", "mp"),
        P(None, "dp", "mp"),
        P(),
        P(),
        P(),
        P(),
    )
    out_specs = (
        P(("dp", "mp"), None, None),
        P(("dp", "mp"), None, None),
        P(None, ("dp", "mp")),
        P(None, ("dp", "mp")),
        P(None, ("dp", "mp")),
        P(None, ("dp", "mp")),
        P(None, ("dp", "mp")),
        P(None, ("dp", "mp")),
        P(None, "dp", "mp"),
        P(None, "dp", "mp"),
        P(None, "dp", "mp"),
        P(None, "dp", "mp"),
        P(None, "dp", "mp"),
        P(None, "dp", "mp"),
        P(),
        P(),
        P(),
        P(),
        P(),
        P(),
    )
    return jax.shard_map(
        per_device, mesh=mesh, in_specs=in_specs, out_specs=out_specs, check_vma=False
    )
```

profile of v0, /device:TPU:0, one launch (start us, length us, event | category | flops | bytes accessed | tf_op | source)
XLA Modules:
  0.0 996.7 jit_solution(14015516016372770413)
XLA Ops:
  14.1 18.3 %gather_fusion.1 = bf16[1072,768]{1,0:T(8,128)(2,1)S(1)} fusion(bf16[4,542,768]{2,0,1:T(4,128)(2,1)} %param.17, s32[1072]{0:T(1024)S(1)} %reshape.324), kind=kCustom, calls=%fused_computation.1 | custom fusion | bytes 3301760 | tf_op jit(solution)/shard_map/jit(take_along_axis)/gather | solution.py:152
  34.2 5.6 convert_element_type.94
  39.8 16.3 %gather_fusion = f32[1072,768]{1,0:T(8,128)S(1)} fusion(f32[4,542,768]{2,0,1:T(4,128)} %convert_element_type.94, s32[1072]{0:T(1024)S(1)} %reshape.324), kind=kCustom, calls=%fused_computation | custom fusion | bytes 6594944 | tf_op jit(solution)/shard_map/jit(take_along_axis)/gather | solution.py:104
  58.2 3.0 select_reduce_fusion
  61.2 3.7 convert_reduce_fusion.1
  65.0 3.3 add_convert_fusion
  68.3 2.5 convert_element_type.96
  70.8 2.8 convolution_reduce_fusion
  77.7 6.5 fusion.17
  86.6 6.1 reshape.362
  92.7 6.9 copy.128
  99.6 6.1 reshape.361
  105.7 7.1 copy.127
  112.8 12.7 %fusion = (f32[4,12,268]{2,1,0:T(8,128)S(1)}, f32[4,12,268,268]{2,3,1,0:T(8,128)}) fusion(pred[268,268]{0,1:T(8,128)(4,1)S(1)} %copy-done.18, bf16[4,268,12,64]{1,3,2,0:T(8,128)(2,1)} %copy.127, bf16[4,268,12,64]{1,3,2,0:T(8,128)(2,1)} %copy.128), kind=kOutput, calls=%fused_computation.11 | convolution fusion | flops 451616448 | bytes 17206672 | tf_op jit(solution)/shard_map/ikhd,ijhd->ihkj/dot_general | solution.py:120
  126.2 12.0 %exponential_reduce_fusion = f32[4,12,268]{2,1,0:T(8,128)} fusion(f32[4,12,268,268]{2,3,1,0:T(8,128)} %get-tuple-element.142, f32[4,12,268]{2,1,0:T(8,128)} %is-finite_select_fusion, pred[268,268]{0,1:T(8,128)(4,1)S(1)} %copy-done.18), kind=kLoop, calls=%fused_computation.7 | loop fusion | flops 13777344 | bytes 13964944 | tf_op jit(solution)/shard_map/reduce_sum | solution.py:122
  138.2 6.1 reshape.360
  144.3 7.3 copy.129
  152.6 12.4 %convert_bitcast_fusion.2 = bf16[4,268,12,64]{1,3,2,0:T(8,128)(2,1)S(1)} fusion(bf16[4,268,12,64]{1,3,2,0:T(8,128)(2,1)} %copy.129, f32[4,12,268,268]{2,3,1,0:T(8,128)} %get-tuple-element.142, f32[4,12,268]{2,1,0:T(8,128)S(1)} %log_add_fusion, pred[268,268]{0,1:T(8,128)(4,1)S(1)} %copy-done.18), kind=kOutput, calls=%fused_computation.84 | convolution fusion | flops 455900160 | bytes 17206672 | tf_op jit(solution)/shard_map/ihkj,ijhd->ikhd/dot_general | solution.py:125
  165.0 3.2 copy.131
  168.3 4.7 convert_element_type.103
  173.0 5.8 fusion.57
  184.0 119.6 %all-gather.7.cloned.1.call-done = bf16[4288,768]{1,0:T(8,128)(2,1)} async-done(((bf16[1072,768]{1,0:T(8,128)(2,1)}), bf16[4288,768]{1,0:T(8,128)(2,1)}) %all-gather.7.cloned.1.call-update) | async-done | bytes 6586384 | tf_op jit(solution)/shard_map/all_gather | solution.py:136
  303.6 38.0 %fusion.3 = (bf16[4288,768]{1,0:T(8,128)(2,1)}, f32[4288,768]{1,0:T(8,128)}) fusion(f32[768]{0:T(1024)S(1)} %dynamic_slice.3, bf16[4288,768]{1,0:T(8,128)(2,1)} %all-gather.7.cloned.1.call-done, bf16[2,768,768]{2,1,0:T(8,128)(2,1)} %all-gather.9.cloned.1.call-done), kind=kOutput, calls=%fused_computation.15 | convolution fusion | flops 5275680768 | bytes 27528192 | tf_op jit(solution)/shard_map/dot_general | solution.py:137
  341.6 81.8 %all-gather.11.cloned.1.call-done = bf16[4288,768]{1,0:T(8,128)(2,1)} async-done(((bf16[1072,768]{1,0:T(8,128)(2,1)}), bf16[4288,768]{1,0:T(8,128)(2,1)}) %all-gather.11.cloned.1.call-update) | async-done | bytes 6586384 | tf_op jit(solution)/shard_map/all_gather | solution.py:155
  423.4 11.5 %convert_reduce_fusion = (f32[768]{0:T(1024)S(1)}, bf16[4288,768]{1,0:T(8,128)(2,1)S(1)}) fusion(f32[4288,768]{1,0:T(8,128)} %get-tuple-element.145, f32[768]{0:T(1024)S(1)} %dynamic_slice.3, bf16[4288,768]{1,0:T(8,128)(2,1)} %all-gather.11.cloned.1.call-done, bf16[2,768,768]{2,1,0:T(8,128)(2,1)S(1)} %copy-done.64), kind=kOutput, calls=%fused_computation.22 | convolution fusion | flops 5101140992 | bytes 27532288 | tf_op jit(solution)/shard_map/dot_general | solution.py:157
  435.0 2.6 copy-done.65
  437.6 8.5 fusion.36
  446.2 9.7 convolution_bitcast_fusion.1
  455.9 9.5 convolution_bitcast_fusion
  467.9 10.1 %convolution_convert_fusion = bf16[4288,768]{1,0:T(8,128)(2,1)} fusion(bf16[4288,768]{1,0:T(8,128)(2,1)} %get-tuple-element.144, bf16[2,768,768]{2,1,0:T(8,128)(2,1)S(1)} %copy-done.64), kind=kOutput, calls=%fused_computation.41 | convolution fusion | flops 5061623808 | bytes 14352384 | tf_op jit(solution)/shard_map/dot_general | solution.py:52
  478.1 187.8 %reduce-scatter.9.cloned.1.call-done = f32[1072,768]{1,0:T(8,128)} async-done(((f32[4288,768]{1,0:T(8,128)}), f32[1072,768]{1,0:T(8,128)}) %reduce-scatter.9.cloned.1.call-update) | async-done | bytes 3293200 | tf_op jit(solution)/shard_map/reduce_scatter | solution.py:162
  665.9 3.4 multiply_reduce_fusion.2
  669.4 3.6 convert_reduce_fusion.2
  674.2 3.9 convolution_convert_fusion.1
  678.1 6.3 reshape.363
  684.4 6.9 copy.133
  691.3 14.5 %convert_bitcast_fusion.1 = bf16[4,268,12,64]{1,3,2,0:T(8,128)(2,1)} fusion(bf16[4,268,12,64]{1,3,2,0:T(8,128)(2,1)} %copy.133, f32[4,12,268,268]{2,3,1,0:T(8,128)} %get-tuple-element.142, f32[4,12,268]{2,1,0:T(8,128)S(1)} %copy-done.26, pred[268,268]{0,1:T(8,128)(4,1)S(1)} %copy-done.19), kind=kOutput, calls=%fused_computation.83 | convolution fusion | flops 455900160 | bytes 17206672 | tf_op jit(solution)/shard_map/ihkj,ikhd->ijhd/dot_general | solution.py:190
  705.8 5.1 copy.143
  710.9 4.7 reshape.313
  715.6 15.3 %multiply_reduce_fusion = (f32[4,12,268]{2,1,0:T(8,128)S(1)}, f32[4,12,268,268]{2,3,1,0:T(8,128)}) fusion(f32[4,12,268,268]{2,3,1,0:T(8,128)} %get-tuple-element.142, f32[4,12,268]{2,1,0:T(8,128)S(1)} %copy-done.26, pred[268,268]{0,1:T(8,128)(4,1)S(1)} %copy-done.19, bf16[4,268,12,64]{1,3,2,0:T(8,128)(2,1)} %copy.133, bf16[4,268,12,64]{1,3,2,0:T(8,128)(2,1)} %copy.129), kind=kOutput, calls=%fused_computation.5 | convolution fusion | flops 458511552 | bytes 31048336 | tf_op jit(solution)/shard_map/ikhd,ijhd->ihkj/dot_general | solution.py:181
  730.8 15.8 %multiply_convert_fusion = bf16[4,12,268,268]{2,3,1,0:T(8,128)(2,1)S(1)} fusion(f32[4,12,268,268]{2,3,1,0:T(8,128)} %get-tuple-element.147, f32[4,12,268,268]{2,3,1,0:T(8,128)} %get-tuple-element.142, f32[4,12,268]{2,1,0:T(8,128)S(1)} %get-tuple-element.146, f32[4,12,268]{2,1,0:T(8,128)S(1)} %copy-done.26, pred[268,268]{0,1:T(8,128)(4,1)S(1)} %copy-done.19), kind=kLoop, calls=%fused_computation.4 | loop fusion | flops 20685312 | bytes 34650256 | tf_op jit(solution)/shard_map/convert_element_type | solution.py:183
  750.5 3.2 copy.137
  753.7 4.9 reshape.311
  758.6 8.3 fusion.29
  766.9 3.2 copy.140
  770.1 4.7 reshape.312
  779.0 3.1 fusion.60
  782.1 6.9 fusion.59
  789.0 8.7 pad_maximum_fusion
  797.7 9.6 copy.153
  808.4 6.8 reshape.317
  815.2 5.8 convert_bitcast_fusion
  821.0 8.4 reshape.321
  829.7 3.0 fusion.53
  834.4 8.3 reduce-scatter.7.cloned.1.call-done
  842.7 13.8 %scatter_custom_fusion = bf16[2168,768]{1,0:T(8,128)(2,1)} fusion(bf16[2168,768]{1,0:T(8,128)(2,1)} %reshape.317, s32[1072]{0:T(1024)S(1)} %reshape.336, f32[1072,768]{1,0:T(8,128)S(1)} %copy-done.2, bf16[1072,768]{1,0:T(8,128)(2,1)} %reduce-scatter.7.cloned.1.call-done, f32[768]{0:T(1024)S(1)} %copy-done.58), kind=kCustom, calls=%fused_computation.87 | custom fusion | flops 3293184 | bytes 8273920
  856.5 6.9 reshape.318
  863.3 8.0 convert_element_type.119
  873.5 10.7 %multiply_reduce_fusion.3 = (f32[768]{0:T(1024)S(1)}, f32[1072]{0:T(1024)S(1)}, f32[1072]{0:T(1024)S(1)}, f32[768]{0:T(1024)S(1)}, f32[1072,768]{1,0:T(8,128)}) fusion(f32[1072]{0:T(1024)S(1)} %copy-done.41, f32[1072]{0:T(1024)S(1)} %copy-done.39, f32[1072,768]{1,0:T(8,128)S(1)} %copy-done.4, pred[1072]{0:T(1024)(128)(4,1)S(1)} %copy-done.48, ...), kind=kOutput, calls=%fused_computation.56 | convolution fusion | flops 3803623936 | bytes 15468528 | tf_op jit(solution)/shard_map/dot_general | solution.py:52
  884.3 17.0 %scatter_custom_fusion.1 = f32[2168,768]{1,0:T(8,128)} fusion(f32[2168,768]{1,0:T(8,128)} %reshape.321, s32[1072]{0:T(1024)S(1)} %reshape.336, f32[1072,768]{1,0:T(8,128)} %get-tuple-element.127, f32[1072,768]{1,0:T(8,128)} %get-tuple-element.148, f32[1072]{0:T(1024)S(1)} %broadcast_multiply_fusion, f32[1072]{0:T(1024)S(1)} %broadcast_multiply_fusion.1, ...), kind=kCustom, calls=%fused_computation.57 | custom fusion | flops 7409664 | bytes 16578560
  901.3 8.3 reshape.322
  909.7 3.6 slice_reduce_fusion
  914.2 41.2 %psum.7 = f32[13,768]{1,0:T(8,128)S(1)} all-reduce(f32[13,768]{1,0:T(8,128)S(1)} %concatenate.21), channel_id=1, replica_groups=mesh['dp'=8,'mp'=4] {'dp','mp'}, use_global_device_ids=true, to_apply=%region_27.28 | all-reduce | flops 9984 | bytes 79872 | tf_op jit(solution)/shard_map/psum | solution.py:242
  956.7 30.2 %reduce-scatter.13.cloned.1.call-done = f32[96,768]{1,0:T(8,128)} async-done(((f32[3072,768]{1,0:T(8,128)}), f32[96,768]{1,0:T(8,128)}) %reduce-scatter.13.cloned.1.call-update) | async-done | bytes 294928
  (213 shorter events, 45.7 us)
Async XLA Ops:
  7.2 70.5 %all-gather.5.cloned.1.call-start = ((), (), s32[]{:S(2)}) async-start(), calls=%async_computation.4 | async-start | bytes 4866048 | tf_op jit(solution)/shard_map/all_gather | solution.py:95
  8.9 175.1 %all-gather.9.cloned.1.call-start = ((), (), s32[]{:S(2)}) async-start(), calls=%async_computation.6 | async-start | bytes 2654208 | tf_op jit(solution)/shard_map/all_gather | solution.py:98
  10.8 292.8 %all-gather.7.cloned.1.call-start = ((), (), s32[]{:S(2)}) async-start(), calls=%async_computation.5 | async-start | bytes 8232960 | tf_op jit(solution)/shard_map/all_gather | solution.py:136
  12.3 61.4 %copy-start.46 = (pred[1072]{0:T(1024)(128)(4,1)}, pred[1072]{0:T(1024)(128)(4,1)S(1)}, u32[]{:S(2)}) copy-start(pred[1072]{0:T(1024)(128)(4,1)S(1)} %broadcast_in_dim.74) | copy-start | bytes 3220
  14.1 59.6 %copy-start.51 = (f32[768]{0:T(1024)}, f32[768]{0:T(1024)S(1)}, u32[]{:S(2)}) copy-start(f32[768]{0:T(1024)S(1)} %get-tuple-element.117) | copy-start | bytes 9220
  32.4 1.8 copy-start.6
  56.1 116.9 %copy-start.3 = (f32[1072,768]{1,0:T(8,128)}, f32[1072,768]{1,0:T(8,128)S(1)}, u32[]{:S(2)}) copy-start(f32[1072,768]{1,0:T(8,128)S(1)} %gather_fusion) | copy-start | bytes 9879556
  61.2 12.5 %copy-start.38 = (f32[1072]{0:T(1024)}, f32[1072]{0:T(1024)S(1)}, u32[]{:S(2)}) copy-start(f32[1072]{0:T(1024)S(1)} %div.41) | copy-start | bytes 12868
  65.0 8.7 copy-start.40
  65.0 5.8 copy-start.31
  73.7 10.6 %copy-start.42 = (f32[1072]{0:T(1024)}, f32[1072]{0:T(1024)S(1)}, u32[]{:S(2)}) copy-start(f32[1072]{0:T(1024)S(1)} %convolution_reduce_fusion) | copy-start | bytes 12868
  73.7 99.3 %copy-start.44 = (f32[1072]{0:T(1024)}, f32[1072]{0:T(1024)S(1)}, u32[]{:S(2)}) copy-start(f32[1072]{0:T(1024)S(1)} %add_divide_fusion) | copy-start | bytes 12868
  105.7 7.1 copy-start.18
  152.5 12.5 %copy-start.25 = (f32[4,12,268]{2,1,0:T(8,128)}, f32[4,12,268]{2,1,0:T(8,128)S(1)}, u32[]{:S(2)}) copy-start(f32[4,12,268]{2,1,0:T(8,128)S(1)} %log_add_fusion) | copy-start | bytes 154372
  165.0 8.0 copy-start.47
  165.0 8.0 copy-start.57
  178.8 1.7 copy-start.1
  178.8 1.7 copy-start.49
  178.8 1.7 copy-start.59
  179.3 3.0 copy-start.7
  182.3 241.1 %all-gather.11.cloned.1.call-start = ((), (), s32[]{:S(2)}) async-start(), calls=%async_computation.8 | async-start | bytes 8232960 | tf_op jit(solution)/shard_map/all_gather | solution.py:155
  183.8 482.1 %reduce-scatter.9.cloned.1.call-start = ((), (), s32[]{:S(2)}) async-start(), calls=%async_computation.9 | async-start | bytes 16465920 | tf_op jit(solution)/shard_map/reduce_scatter | solution.py:162
  184.0 239.4 %copy-start.64 = (bf16[2,768,768]{2,1,0:T(8,128)(2,1)S(1)}, bf16[2,768,768]{2,1,0:T(8,128)(2,1)}, u32[]{:S(2)}) copy-start(bf16[2,768,768]{2,1,0:T(8,128)(2,1)} %all-gather.9.cloned.1.call-done) | copy-start | bytes 7077892
  434.9 2.7 copy-start.65
  446.1 383.5 %reduce-scatter.11.cloned.1.call-start = ((), (), s32[]{:S(2)}) async-start(), calls=%async_computation.10 | async-start | bytes 5308416 | tf_op jit(solution)/shard_map/reduce_scatter | solution.py:222
  467.9 374.8 %reduce-scatter.7.cloned.1.call-start = ((), (), s32[]{:S(2)}) async-start(), calls=%async_computation.7 | async-start | bytes 8232960 | tf_op jit(solution)/shard_map/reduce_scatter | solution.py:140
  478.0 187.9 %copy-start.2 = (f32[1072,768]{1,0:T(8,128)S(1)}, f32[1072,768]{1,0:T(8,128)}, u32[]{:S(2)}) copy-start(f32[1072,768]{1,0:T(8,128)} %copy-done.1) | copy-start | bytes 9879556
  478.0 187.9 %copy-start.35 = (f32[1072]{0:T(1024)S(1)}, f32[1072]{0:T(1024)}, u32[]{:S(2)}) copy-start(f32[1072]{0:T(1024)} %copy-done.34) | copy-start | bytes 12868
  478.0 187.9 %copy-start.37 = (f32[1072]{0:T(1024)S(1)}, f32[1072]{0:T(1024)}, u32[]{:S(2)}) copy-start(f32[1072]{0:T(1024)} %copy-done.36) | copy-start | bytes 12868
  478.0 187.9 %copy-start.50 = (f32[768]{0:T(1024)S(1)}, f32[768]{0:T(1024)}, u32[]{:S(2)}) copy-start(f32[768]{0:T(1024)} %get-tuple-element.112) | copy-start | bytes 9220
  478.1 191.3 %copy-start.45 = (f32[1072]{0:T(1024)S(1)}, f32[1072]{0:T(1024)}, u32[]{:S(2)}) copy-start(f32[1072]{0:T(1024)} %copy-done.44) | copy-start | bytes 12868
  478.1 191.3 %copy-start.48 = (pred[1072]{0:T(1024)(128)(4,1)S(1)}, pred[1072]{0:T(1024)(128)(4,1)}, u32[]{:S(2)}) copy-start(pred[1072]{0:T(1024)(128)(4,1)} %copy-done.46) | copy-start | bytes 3220
  478.1 508.9 %reduce-scatter.13.cloned.1.call-start = ((), (), s32[]{:S(2)}) async-start(), calls=%async_computation.11 | async-start | bytes 9732096
  665.9 3.5 copy-start.8
  665.9 3.5 copy-start.11
  684.4 6.9 copy-start.19
  684.4 7.0 copy-start.26
  730.8 15.8 %copy-start.9 = (bf16[4,268,12,64]{1,3,2,0:T(8,128)(2,1)S(1)}, bf16[4,268,12,64]{1,3,2,0:T(8,128)(2,1)}, u32[]{:S(2)}) copy-start(bf16[4,268,12,64]{1,3,2,0:T(8,128)(2,1)} %copy.128) | copy-start | bytes 4939780
  746.6 3.8 copy-start
  774.8 2.0 copy-start.15
  774.8 2.5 copy-start.14
  776.8 2.2 copy-start.22
  779.0 3.1 copy-start.12
  779.0 3.1 copy-start.16
  808.3 6.9 copy-start.60
  829.4 13.3 %copy-start.58 = (f32[768]{0:T(1024)S(1)}, f32[768]{0:T(1024)}, u32[]{:S(2)}) copy-start(f32[768]{0:T(1024)} %get-tuple-element.118) | copy-start | bytes 9220
  829.7 3.9 copy-start.27
  863.3 8.1 copy-start.5
  863.3 8.1 copy-start.10
  871.4 2.1 copy-start.4
  871.4 2.1 copy-start.39
  871.4 2.1 copy-start.41
  871.4 2.1 copy-start.52
  871.4 2.1 copy-start.61
  909.6 3.7 copy-start.17
  909.6 46.4 %copy-start.32 = (f32[13,768]{1,0:T(8,128)S(1)}, f32[13,768]{1,0:T(8,128)}, u32[]{:S(2)}) copy-start(f32[13,768]{1,0:T(8,128)} %param.27) | copy-start | bytes 119812
  909.6 46.4 %copy-start.54 = (f32[13,768]{1,0:T(8,128)S(1)}, f32[13,768]{1,0:T(8,128)}, u32[]{:S(2)}) copy-start(f32[13,768]{1,0:T(8,128)} %param.30) | copy-start | bytes 119812
  909.6 46.4 %copy-start.55 = (f32[13,768]{1,0:T(8,128)S(1)}, f32[13,768]{1,0:T(8,128)}, u32[]{:S(2)}) copy-start(f32[13,768]{1,0:T(8,128)} %param.29) | copy-start | bytes 119812
  909.7 46.4 %copy-start.56 = (f32[13,768]{1,0:T(8,128)S(1)}, f32[13,768]{1,0:T(8,128)}, u32[]{:S(2)}) copy-start(f32[13,768]{1,0:T(8,128)} %param.28) | copy-start | bytes 119812
  909.7 77.3 %copy-start.24 = (f32[768,96]{0,1:T(8,128)S(1)}, f32[768,96]{0,1:T(8,128)}, u32[]{:S(2)}) copy-start(f32[768,96]{0,1:T(8,128)} %param.19) | copy-start | bytes 884740
  909.7 77.3 %copy-start.28 = (f32[768,96]{0,1:T(8,128)S(1)}, f32[768,96]{0,1:T(8,128)}, u32[]{:S(2)}) copy-start(f32[768,96]{0,1:T(8,128)} %param.21) | copy-start | bytes 884740
  909.7 77.3 %copy-start.29 = (f32[768,96]{0,1:T(8,128)S(1)}, f32[768,96]{0,1:T(8,128)}, u32[]{:S(2)}) copy-start(f32[768,96]{0,1:T(8,128)} %param.20) | copy-start | bytes 884740
  913.3 75.6 %copy-start.30 = (f32[768,96]{0,1:T(8,128)S(1)}, f32[768,96]{0,1:T(8,128)}, u32[]{:S(2)}) copy-start(f32[768,96]{0,1:T(8,128)} %param.22) | copy-start | bytes 884740
  955.4 34.3 %copy-start.33 = (f32[13,768]{1,0:T(8,128)}, f32[13,768]{1,0:T(8,128)S(1)}, u32[]{:S(2)}) copy-start(f32[13,768]{1,0:T(8,128)S(1)} %psum.7) | copy-start | bytes 119812
  (10 other events, 10.2 us)
Sparse Core Ops, SparseCore 0:
  11.4 66.2 all-gather.4
  80.2 27.8 all-gather.8
  182.4 121.1 all-gather.6
  305.0 118.3 all-gather.10
  446.3 219.5 reduce-scatter.8
  669.8 54.9 reduce-scatter.10
  727.2 115.4 reduce-scatter.6
  850.2 136.7 reduce-scatter.12
where the time goes:
time: 1010 us; the launch traced here: 997 us
  waiting for transfers between devices  430 us (43%)
  matrix products  194 us (19%)
  local copies, waits for them, and re-layouts  187 us (19%)
  other arithmetic  130 us (13%)
  blocking collectives  41.2 us (4%)
  between operations  15.1 us (1%)
    reduce_scatter x1, waiting for transfers between devices, per_device(): lax.psum_scatter(product_transposed(piece, feed_rows[0]), 'mp', scatter_d...  188 us
    all_gather x1, waiting for transfers between devices, per_device(): rows_all = lax.all_gather(normed_two, 'mp', axis=0, tiled=True)  120 us
    all_gather x1, waiting for transfers between devices, per_device(): cot_all = lax.all_gather(cot_kept, 'mp', axis=0, tiled=True)  81.8 us
    unnamed x140, local copies, waits for them, and re-layouts  53.9 us
    psum x1, blocking collectives, per_device(): vector_gradient = lax.psum(vector_local, ('dp', 'mp'))  41.2 us
    dot_general x1, matrix products, per_device(): jnp.dot(rows_all, feed_rows[0], preferred_element_type=f32) + bias_used  38 us
    unnamed x6, other arithmetic  36.7 us
    dot_general x4, matrix products, product_transposed(): lax.dot_general(left, right, (((1,), (1,)), ((), ())), preferred_element_...  33.3 us
  transfers between devices with their start and end apart: 8, of which 6 were waited for; matrix products, arithmetic and copies ran while one was open for 48% of the time, Pallas kernels for 0%

commit v1 on v0

--- a/solution.py
+++ b/solution.py
@@ -239,7 +239,8 @@
         ],
         axis=0,
     )
-    vector_gradient = lax.psum(vector_local, ("dp", "mp"))
+    parts = lax.all_gather(vector_local, ("dp", "mp"), axis=0, tiled=False)
+    vector_gradient = parts.sum(axis=0)
     attention_new = adamw(
         attention_gradient,
         attention_first,

time: 1010 us -> 1060 us (1.050)
  waiting for transfers between devices: 430 us -> 522 us
  blocking collectives: 41.2 us -> 0 us
  local copies, waits for them, and re-layouts: 187 us -> 200 us
  other arithmetic: 130 us -> 118 us
    unnamed x9 -> x10, waiting for transfers between devices: 30.4 us -> 139 us
    psum x1 -> x0, blocking collectives: 41.2 us -> none  [per_device(): vector_gradient = lax.psum(vector_local, ('dp', 'mp'))]
    gather x2, local copies, waits for them, and re-layouts: 18.4 us -> 29.4 us  [per_device(): jnp.take_along_axis(tokens_float, kept_index[:, :, None], axis=1)]
  transfers between devices with their start and end apart: 8 -> 9, of which waited for: 6 -> 5; matrix products, arithmetic and copies ran while one was open for 48% -> 45% of each run, Pallas kernels for 0% -> 0%
where the time goes in v1:
time: 1060 us; the launch traced here: 1050 us
  waiting for transfers between devices  522 us (49%)
  local copies, waits for them, and re-layouts  200 us (19%)
  matrix products  198 us (19%)
  other arithmetic  118 us (11%)
  between operations  14.9 us (1%)
    reduce_scatter x1, waiting for transfers between devices, per_device(): lax.psum_scatter(product_transposed(piece, feed_rows[0]), 'mp', scatter_d...  185 us
    unnamed x10, waiting for transfers between devices  139 us
    all_gather x1, waiting for transfers between devices, per_device(): rows_all = lax.all_gather(normed_two, 'mp', axis=0, tiled=True)  113 us
    all_gather x1, waiting for transfers between devices, per_device(): cot_all = lax.all_gather(cot_kept, 'mp', axis=0, tiled=True)  81.6 us
    unnamed x140, local copies, waits for them, and re-layouts  58.3 us
    dot_general x1, matrix products, per_device(): jnp.dot(rows_all, feed_rows[0], preferred_element_type=f32) + bias_used  38.2 us
    unnamed x6, other arithmetic  36.2 us
    dot_general x4, matrix products, transpose_product(): lax.dot_general(left, right, (((0,), (0,)), ((), ())), preferred_element_...  34.1 us
  transfers between devices with their start and end apart: 9, of which 5 were waited for; matrix products, arithmetic and copies ran while one was open for 45% of the time, Pallas kernels for 0%

profile of v1, /device:TPU:0, one launch (start us, length us, event | category | flops | bytes accessed | tf_op | source)
XLA Modules:
  0.0 1053.6 jit_solution(4181431639071301422)
XLA Ops:
  14.1 23.7 %gather_fusion.1 = bf16[1072,768]{1,0:T(8,128)(2,1)S(1)} fusion(bf16[4,542,768]{2,0,1:T(4,128)(2,1)} %param.17, s32[1072]{0:T(1024)S(1)} %reshape.324), kind=kCustom, calls=%fused_computation.1 | custom fusion | bytes 3301760 | tf_op jit(solution)/shard_map/jit(take_along_axis)/gather | solution.py:152
  39.5 5.6 convert_element_type.94
  45.1 26.1 %gather_fusion = f32[1072,768]{1,0:T(8,128)} fusion(f32[4,542,768]{2,0,1:T(4,128)} %convert_element_type.94, s32[1072]{0:T(1024)S(1)} %reshape.324), kind=kCustom, calls=%fused_computation | custom fusion | bytes 6594944 | tf_op jit(solution)/shard_map/jit(take_along_axis)/gather | solution.py:104
  71.2 3.3 reshape.327
  74.5 2.6 select_reduce_fusion
  77.3 3.2 convert_reduce_fusion.1
  80.5 3.3 add_convert_fusion
  83.8 2.6 convert_element_type.96
  86.4 2.9 convolution_reduce_fusion
  90.1 2.4 add_convert_fusion.3
  92.5 6.6 fusion.17
  100.6 3.9 reshape.366
  104.5 6.9 copy.128
  111.4 3.9 reshape.365
  115.3 6.2 copy.127
  121.6 12.9 %fusion = (f32[4,12,268]{2,1,0:T(8,128)S(1)}, f32[4,12,268,268]{2,3,1,0:T(8,128)}) fusion(pred[268,268]{0,1:T(8,128)(4,1)S(1)} %copy-done.21, bf16[4,268,12,64]{1,3,2,0:T(8,128)(2,1)S(1)} %copy.127, bf16[4,268,12,64]{1,3,2,0:T(8,128)(2,1)} %copy.128), kind=kOutput, calls=%fused_computation.11 | convolution fusion | flops 451616448 | bytes 17206672 | tf_op jit(solution)/shard_map/ikhd,ijhd->ihkj/dot_general | solution.py:120
  134.5 11.7 %exponential_reduce_fusion = f32[4,12,268]{2,1,0:T(8,128)S(1)} fusion(f32[4,12,268,268]{2,3,1,0:T(8,128)} %get-tuple-element.142, f32[4,12,268]{2,1,0:T(8,128)S(1)} %is-finite_select_fusion, pred[268,268]{0,1:T(8,128)(4,1)S(1)} %copy-done.21), kind=kLoop, calls=%fused_computation.7 | loop fusion | flops 13777344 | bytes 13964944 | tf_op jit(solution)/shard_map/reduce_sum | solution.py:122
  146.2 3.9 reshape.364
  150.2 6.3 copy.129
  156.5 12.6 %convert_bitcast_fusion.2 = bf16[4,268,12,64]{1,3,2,0:T(8,128)(2,1)S(1)} fusion(bf16[4,268,12,64]{1,3,2,0:T(8,128)(2,1)S(1)} %copy.129, f32[4,12,268,268]{2,3,1,0:T(8,128)} %get-tuple-element.142, f32[4,12,268]{2,1,0:T(8,128)S(1)} %log_add_fusion, pred[268,268]{0,1:T(8,128)(4,1)S(1)} %copy-done.21), kind=kOutput, calls=%fused_computation.84 | convolution fusion | flops 455900160 | bytes 17206672 | tf_op jit(solution)/shard_map/ihkj,ijhd->ikhd/dot_general | solution.py:125
  169.1 3.2 copy.131
  172.3 4.7 convert_element_type.103
  177.0 6.7 fusion.57
  187.3 2.8 broadcast_select_fusion
  190.4 113.1 %all-gather.10.cloned.1.call-done = bf16[4288,768]{1,0:T(8,128)(2,1)} async-done(((bf16[1072,768]{1,0:T(8,128)(2,1)}), bf16[4288,768]{1,0:T(8,128)(2,1)}) %all-gather.10.cloned.1.call-update) | async-done | bytes 6586384 | tf_op jit(solution)/shard_map/all_gather | solution.py:136
  303.5 38.2 %fusion.3 = (bf16[4288,768]{1,0:T(8,128)(2,1)}, f32[4288,768]{1,0:T(8,128)}) fusion(f32[768]{0:T(1024)S(1)} %dynamic_slice.3, bf16[4288,768]{1,0:T(8,128)(2,1)} %all-gather.10.cloned.1.call-done, bf16[2,768,768]{2,1,0:T(8,128)(2,1)} %all-gather.12.cloned.1.call-done), kind=kOutput, calls=%fused_computation.15 | convolution fusion | flops 5275680768 | bytes 27528192 | tf_op jit(solution)/shard_map/dot_general | solution.py:137
  341.7 81.6 %all-gather.14.cloned.1.call-done = bf16[4288,768]{1,0:T(8,128)(2,1)} async-done(((bf16[1072,768]{1,0:T(8,128)(2,1)}), bf16[4288,768]{1,0:T(8,128)(2,1)}) %all-gather.14.cloned.1.call-update) | async-done | bytes 6586384 | tf_op jit(solution)/shard_map/all_gather | solution.py:155
  423.3 11.5 %convert_reduce_fusion = (f32[768]{0:T(1024)S(1)}, bf16[4288,768]{1,0:T(8,128)(2,1)S(1)}) fusion(f32[4288,768]{1,0:T(8,128)} %get-tuple-element.145, f32[768]{0:T(1024)S(1)} %dynamic_slice.3, bf16[4288,768]{1,0:T(8,128)(2,1)} %all-gather.14.cloned.1.call-done, bf16[2,768,768]{2,1,0:T(8,128)(2,1)S(1)} %copy-done.63), kind=kOutput, calls=%fused_computation.22 | convolution fusion | flops 5101140992 | bytes 27532288 | tf_op jit(solution)/shard_map/dot_general | solution.py:157
  434.8 2.6 copy-done.65
  437.5 8.5 fusion.36
  446.1 9.7 convolution_bitcast_fusion.1
  455.8 9.5 convolution_bitcast_fusion
  469.4 10.1 convolution_convert_fusion
  480.5 185.3 %reduce-scatter.9.cloned.1.call-done = f32[1072,768]{1,0:T(8,128)} async-done(((f32[4288,768]{1,0:T(8,128)}), f32[1072,768]{1,0:T(8,128)}) %reduce-scatter.9.cloned.1.call-update) | async-done | bytes 3293200 | tf_op jit(solution)/shard_map/reduce_scatter | solution.py:162
  665.8 3.4 multiply_reduce_fusion.2
  673.5 3.9 convolution_convert_fusion.1
  677.4 6.3 reshape.367
  683.7 7.1 copy.133
  690.9 14.5 %convert_bitcast_fusion.1 = bf16[4,268,12,64]{1,3,2,0:T(8,128)(2,1)} fusion(bf16[4,268,12,64]{1,3,2,0:T(8,128)(2,1)} %copy.133, f32[4,12,268,268]{2,3,1,0:T(8,128)} %get-tuple-element.142, f32[4,12,268]{2,1,0:T(8,128)S(1)} %copy-done.28, pred[268,268]{0,1:T(8,128)(4,1)S(1)} %copy-done.22), kind=kOutput, calls=%fused_computation.83 | convolution fusion | flops 455900160 | bytes 17206672 | tf_op jit(solution)/shard_map/ihkj,ikhd->ijhd/dot_general | solution.py:190
  705.4 4.9 copy.143
  710.3 4.7 reshape.313
  715.0 15.1 %multiply_reduce_fusion = (f32[4,12,268]{2,1,0:T(8,128)S(1)}, f32[4,12,268,268]{2,3,1,0:T(8,128)}) fusion(f32[4,12,268,268]{2,3,1,0:T(8,128)} %get-tuple-element.142, f32[4,12,268]{2,1,0:T(8,128)S(1)} %copy-done.28, pred[268,268]{0,1:T(8,128)(4,1)S(1)} %copy-done.22, bf16[4,268,12,64]{1,3,2,0:T(8,128)(2,1)} %copy.133, bf16[4,268,12,64]{1,3,2,0:T(8,128)(2,1)} %copy-done.13), kind=kOutput, calls=%fused_computation.5 | convolution fusion | flops 458511552 | bytes 31048336 | tf_op jit(solution)/shard_map/ikhd,ijhd->ihkj/dot_general | solution.py:181
  730.1 16.2 %multiply_convert_fusion = bf16[4,12,268,268]{2,3,1,0:T(8,128)(2,1)S(1)} fusion(f32[4,12,268,268]{2,3,1,0:T(8,128)} %get-tuple-element.147, f32[4,12,268,268]{2,3,1,0:T(8,128)} %get-tuple-element.142, f32[4,12,268]{2,1,0:T(8,128)S(1)} %get-tuple-element.146, f32[4,12,268]{2,1,0:T(8,128)S(1)} %copy-done.28, pred[268,268]{0,1:T(8,128)(4,1)S(1)} %copy-done.22), kind=kLoop, calls=%fused_computation.4 | loop fusion | flops 20685312 | bytes 34650256 | tf_op jit(solution)/shard_map/convert_element_type | solution.py:183
  746.3 2.4 fusion.28
  750.2 3.2 copy.137
  753.4 4.7 reshape.311
  758.1 8.3 fusion.29
  766.4 3.2 copy.140
  769.6 4.8 reshape.312
  781.2 9.0 multiply_reduce_fusion.3
  793.7 5.2 fusion.60
  798.9 9.7 fusion.59
  808.6 8.8 pad_maximum_fusion
  817.4 9.7 copy.153
  828.0 6.4 reshape.317
  834.5 5.6 convert_bitcast_fusion
  840.1 8.4 reshape.321
  848.5 3.0 fusion.53
  853.3 13.8 %scatter_custom_fusion = bf16[2168,768]{1,0:T(8,128)(2,1)} fusion(bf16[2168,768]{1,0:T(8,128)(2,1)} %reshape.317, s32[1072]{0:T(1024)S(1)} %reshape.336, f32[1072,768]{1,0:T(8,128)S(1)} %copy-done.2, bf16[1072,768]{1,0:T(8,128)(2,1)} %reduce-scatter.7.cloned.1.call-done, f32[768]{0:T(1024)S(1)} %copy-done.58), kind=kCustom, calls=%fused_computation.87 | custom fusion | flops 3293184 | bytes 8273920
  867.1 7.1 reshape.318
  874.2 16.6 %scatter_custom_fusion.1 = f32[2168,768]{1,0:T(8,128)} fusion(f32[2168,768]{1,0:T(8,128)} %reshape.321, s32[1072]{0:T(1024)S(1)} %reshape.336, f32[1072,768]{1,0:T(8,128)} %copy-done.6, f32[1072,768]{1,0:T(8,128)} %get-tuple-element.148, f32[1072]{0:T(1024)S(1)} %broadcast_multiply_fusion, f32[1072]{0:T(1024)S(1)} %broadcast_multiply_fusion.1, ...), kind=kCustom, calls=%fused_computation.57 | custom fusion | flops 7409664 | bytes 16578560
  890.8 8.4 reshape.322
  899.2 2.9 all-gather.16.cloned.1.call-done
  904.9 139.2 %reduce-scatter.13.cloned.1.call-done = f32[96,768]{1,0:T(8,128)} async-done(((f32[3072,768]{1,0:T(8,128)}), f32[96,768]{1,0:T(8,128)}) %reduce-scatter.13.cloned.1.call-update) | async-done | bytes 294928
  (216 shorter events, 43.7 us)
Async XLA Ops:
  7.2 85.3 %all-gather.8.cloned.1.call-start = ((), (), s32[]{:S(2)}) async-start(), calls=%async_computation.4 | async-start | bytes 4866048 | tf_op jit(solution)/shard_map/all_gather | solution.py:95
  8.9 181.5 %all-gather.12.cloned.1.call-start = ((), (), s32[]{:S(2)}) async-start(), calls=%async_computation.6 | async-start | bytes 2654208 | tf_op jit(solution)/shard_map/all_gather | solution.py:98
  10.8 292.7 %all-gather.10.cloned.1.call-start = ((), (), s32[]{:S(2)}) async-start(), calls=%async_computation.5 | async-start | bytes 8232960 | tf_op jit(solution)/shard_map/all_gather | solution.py:136
  12.3 175.0 %copy-start.48 = (pred[1072]{0:T(1024)(128)(4,1)}, pred[1072]{0:T(1024)(128)(4,1)S(1)}, u32[]{:S(2)}) copy-start(pred[1072]{0:T(1024)(128)(4,1)S(1)} %broadcast_in_dim.74) | copy-start | bytes 3220
  14.1 75.9 %copy-start.52 = (f32[768]{0:T(1024)}, f32[768]{0:T(1024)S(1)}, u32[]{:S(2)}) copy-start(f32[768]{0:T(1024)S(1)} %get-tuple-element.117) | copy-start | bytes 9220
  14.1 170.1 %copy-start.50 = (f32[768]{0:T(1024)}, f32[768]{0:T(1024)S(1)}, u32[]{:S(2)}) copy-start(f32[768]{0:T(1024)S(1)} %get-tuple-element.112) | copy-start | bytes 9220
  37.8 7.2 copy-start.8
  74.5 2.7 copy-start.17
  77.2 12.8 %copy-start.40 = (f32[1072]{0:T(1024)}, f32[1072]{0:T(1024)S(1)}, u32[]{:S(2)}) copy-start(f32[1072]{0:T(1024)S(1)} %div.41) | copy-start | bytes 12868
  80.5 9.5 copy-start.42
  80.5 5.9 copy-start.33
  83.8 6.2 copy-start.3
  90.0 87.0 %copy-start.46 = (f32[1072]{0:T(1024)}, f32[1072]{0:T(1024)S(1)}, u32[]{:S(2)}) copy-start(f32[1072]{0:T(1024)S(1)} %add_divide_fusion) | copy-start | bytes 12868
  115.3 6.3 copy-start.21
  121.6 12.9 %copy-start.7 = (bf16[4,268,12,64]{1,3,2,0:T(8,128)(2,1)}, bf16[4,268,12,64]{1,3,2,0:T(8,128)(2,1)S(1)}, u32[]{:S(2)}) copy-start(bf16[4,268,12,64]{1,3,2,0:T(8,128)(2,1)S(1)} %copy.127) | copy-start | bytes 4939780
  134.5 11.7 %copy-start.20 = (bf16[1072,768]{1,0:T(8,128)(2,1)S(1)}, bf16[1072,768]{1,0:T(8,128)(2,1)}, u32[]{:S(2)}) copy-start(bf16[1072,768]{1,0:T(8,128)(2,1)} %get-tuple-element.140) | copy-start | bytes 4939780
  156.4 12.6 %copy-start.13 = (bf16[4,268,12,64]{1,3,2,0:T(8,128)(2,1)}, bf16[4,268,12,64]{1,3,2,0:T(8,128)(2,1)S(1)}, u32[]{:S(2)}) copy-start(bf16[4,268,12,64]{1,3,2,0:T(8,128)(2,1)S(1)} %copy.129) | copy-start | bytes 4939780
  156.5 12.6 %copy-start.27 = (f32[4,12,268]{2,1,0:T(8,128)}, f32[4,12,268]{2,1,0:T(8,128)S(1)}, u32[]{:S(2)}) copy-start(f32[4,12,268]{2,1,0:T(8,128)S(1)} %log_add_fusion) | copy-start | bytes 154372
  183.7 1.8 copy-start.1
  187.3 236.1 %all-gather.14.cloned.1.call-start = ((), (), s32[]{:S(2)}) async-start(), calls=%async_computation.8 | async-start | bytes 8232960 | tf_op jit(solution)/shard_map/all_gather | solution.py:155
  190.2 475.6 %reduce-scatter.9.cloned.1.call-start = ((), (), s32[]{:S(2)}) async-start(), calls=%async_computation.9 | async-start | bytes 16465920 | tf_op jit(solution)/shard_map/reduce_scatter | solution.py:162
  190.4 233.0 %copy-start.63 = (bf16[2,768,768]{2,1,0:T(8,128)(2,1)S(1)}, bf16[2,768,768]{2,1,0:T(8,128)(2,1)}, u32[]{:S(2)}) copy-start(bf16[2,768,768]{2,1,0:T(8,128)(2,1)} %all-gather.12.cloned.1.call-done) | copy-start | bytes 7077892
  434.8 2.7 copy-start.65
  446.0 402.5 %reduce-scatter.11.cloned.1.call-start = ((), (), s32[]{:S(2)}) async-start(), calls=%async_computation.10 | async-start | bytes 5308416 | tf_op jit(solution)/shard_map/reduce_scatter | solution.py:222
  467.7 385.6 %reduce-scatter.7.cloned.1.call-start = ((), (), s32[]{:S(2)}) async-start(), calls=%async_computation.7 | async-start | bytes 8232960 | tf_op jit(solution)/shard_map/reduce_scatter | solution.py:140
  479.5 186.3 %copy-start.2 = (f32[1072,768]{1,0:T(8,128)S(1)}, f32[1072,768]{1,0:T(8,128)}, u32[]{:S(2)}) copy-start(f32[1072,768]{1,0:T(8,128)} %copy-done.1) | copy-start | bytes 9879556
  479.5 186.3 %copy-start.37 = (f32[1072]{0:T(1024)S(1)}, f32[1072]{0:T(1024)}, u32[]{:S(2)}) copy-start(f32[1072]{0:T(1024)} %copy-done.36) | copy-start | bytes 12868
  479.5 186.3 %copy-start.39 = (f32[1072]{0:T(1024)S(1)}, f32[1072]{0:T(1024)}, u32[]{:S(2)}) copy-start(f32[1072]{0:T(1024)} %copy-done.38) | copy-start | bytes 12868
  479.5 186.3 %copy-start.51 = (f32[768]{0:T(1024)S(1)}, f32[768]{0:T(1024)}, u32[]{:S(2)}) copy-start(f32[768]{0:T(1024)} %copy-done.50) | copy-start | bytes 9220
  479.6 422.5 %all-gather.16.cloned.1.call-start = ((), (), s32[]{:S(2)}) async-start(), calls=%async_computation.11 | async-start | bytes 1622016 | tf_op jit(solution)/shard_map/all_gather | solution.py:242
  480.5 188.8 %copy-start.47 = (f32[1072]{0:T(1024)S(1)}, f32[1072]{0:T(1024)}, u32[]{:S(2)}) copy-start(f32[1072]{0:T(1024)} %copy-done.46) | copy-start | bytes 12868
  480.5 188.8 %copy-start.49 = (pred[1072]{0:T(1024)(128)(4,1)S(1)}, pred[1072]{0:T(1024)(128)(4,1)}, u32[]{:S(2)}) copy-start(pred[1072]{0:T(1024)(128)(4,1)} %copy-done.48) | copy-start | bytes 3220
  665.8 3.5 copy-start.9
  665.8 3.5 copy-start.12
  669.3 3.7 copy-start.11
  671.2 1.8 copy-start.6
  671.2 2.3 copy-start.24
  671.2 2.2 copy-start.45
  683.7 7.1 copy-start.22
  683.7 7.2 copy-start.28
  730.1 16.2 %copy-start.10 = (bf16[4,268,12,64]{1,3,2,0:T(8,128)(2,1)S(1)}, bf16[4,268,12,64]{1,3,2,0:T(8,128)(2,1)}, u32[]{:S(2)}) copy-start(bf16[4,268,12,64]{1,3,2,0:T(8,128)(2,1)} %copy.128) | copy-start | bytes 4939780
  746.3 3.8 copy-start
  774.5 2.0 copy-start.16
  774.5 2.5 copy-start.15
  777.3 2.7 copy-start.14
  777.3 3.9 copy-start.4
  777.3 3.9 copy-start.41
  777.3 3.8 copy-start.43
  777.3 3.8 copy-start.53
  777.3 3.8 copy-start.60
  793.6 250.4 %reduce-scatter.13.cloned.1.call-start = ((), (), s32[]{:S(2)}) async-start(), calls=%async_computation.12 | async-start | bytes 9732096
  793.7 5.2 copy-start.19
  848.5 4.8 copy-start.58
  848.5 3.9 copy-start.29
  867.1 7.1 copy-start.5
  890.7 13.4 %copy-start.34 = (f32[13,768]{1,0:T(8,128)S(1)}, f32[13,768]{1,0:T(8,128)}, u32[]{:S(2)}) copy-start(f32[13,768]{1,0:T(8,128)} %param.27) | copy-start | bytes 119812
  890.7 13.4 %copy-start.55 = (f32[13,768]{1,0:T(8,128)S(1)}, f32[13,768]{1,0:T(8,128)}, u32[]{:S(2)}) copy-start(f32[13,768]{1,0:T(8,128)} %param.30) | copy-start | bytes 119812
  890.7 13.4 %copy-start.56 = (f32[13,768]{1,0:T(8,128)S(1)}, f32[13,768]{1,0:T(8,128)}, u32[]{:S(2)}) copy-start(f32[13,768]{1,0:T(8,128)} %param.29) | copy-start | bytes 119812
  890.7 13.4 %copy-start.57 = (f32[13,768]{1,0:T(8,128)S(1)}, f32[13,768]{1,0:T(8,128)}, u32[]{:S(2)}) copy-start(f32[13,768]{1,0:T(8,128)} %param.28) | copy-start | bytes 119812
  890.7 153.3 %copy-start.26 = (f32[768,96]{0,1:T(8,128)S(1)}, f32[768,96]{0,1:T(8,128)}, u32[]{:S(2)}) copy-start(f32[768,96]{0,1:T(8,128)} %param.19) | copy-start | bytes 884740
  890.8 153.3 %copy-start.30 = (f32[768,96]{0,1:T(8,128)S(1)}, f32[768,96]{0,1:T(8,128)}, u32[]{:S(2)}) copy-start(f32[768,96]{0,1:T(8,128)} %param.21) | copy-start | bytes 884740
  890.8 153.3 %copy-start.31 = (f32[768,96]{0,1:T(8,128)S(1)}, f32[768,96]{0,1:T(8,128)}, u32[]{:S(2)}) copy-start(f32[768,96]{0,1:T(8,128)} %param.20) | copy-start | bytes 884740
  899.2 146.8 %copy-start.32 = (f32[768,96]{0,1:T(8,128)S(1)}, f32[768,96]{0,1:T(8,128)}, u32[]{:S(2)}) copy-start(f32[768,96]{0,1:T(8,128)} %param.22) | copy-start | bytes 884740
  903.5 143.3 %copy-start.35 = (f32[13,768]{1,0:T(8,128)}, f32[13,768]{1,0:T(8,128)S(1)}, u32[]{:S(2)}) copy-start(f32[13,768]{1,0:T(8,128)S(1)} %reduce_sum.209) | copy-start | bytes 119812
  (11 other events, 11.3 us)
Sparse Core Ops, SparseCore 0:
  11.4 66.2 all-gather.7
  80.2 27.8 all-gather.11
  187.4 116.0 all-gather.9
  304.9 118.3 all-gather.13
  446.2 219.5 reduce-scatter.8
  669.7 54.8 reduce-scatter.10
  727.0 115.4 reduce-scatter.6
  846.4 55.5 all-gather.15
  909.5 134.4 reduce-scatter.12
